TPU v7x, 768 devices: a whole 4x8x12 slice. The times are simulated.
768 devices in a mesh: batch: 192 (over y_lo, z, x), rep: 4 (over y_hi, core).
Axes of the slice: x: 4, y: 8 (y_hi: 2, y_lo: 4; y = y_hi * 4 + y_lo), z: 12, core: 2. Of those that a mesh axis runs over, the one named last changes fastest.
Arguments:
- feats: bfloat16 [24576, 512], P('batch')
- partner: int32 [24576], P('batch'), may hold values from 0 to 24575, as said below
Outputs:
- grad: float32 [24576, 512], P('batch')
- loss: float32 [24576], P('batch')
Inputs may be any that keep to these rules, and one draw needn't show every extreme that they name: partner pairs the rows: partner[partner[k]] = k and partner[k] != k.
All inputs are finite; a program needn't handle non-finite values.
Results may differ from a plain program's by a relative error of at most 0.0058.
Values may be sent and summed in bfloat16 or wider, within the bound.
A program may use at most 32 MiB of HBM per device.

v0:
```python
import math

import jax
import jax.numpy as jnp
from jax import lax
from jax.sharding import PartitionSpec as P

inv_temp = 10.0


def on_device(feats, partner):
    rows, width = feats.shape
    layers = lax.axis_size("rep")
    share = rows // layers
    layer = lax.axis_index("rep")
    block_index = lax.axis_index("batch")
    hf = feats.astype(jnp.float32)
    scale = lax.rsqrt(jnp.sum(hf * hf, axis=-1, keepdims=True) + 1e-06)
    unit = hf * scale
    embed = unit.astype(jnp.bfloat16)
    own_ids = block_index * rows + jnp.arange(rows, dtype=jnp.int32)
    mine = lax.dynamic_slice_in_dim(embed, layer * share, share, 0)

    def key_ids(start, count):
        gathered = start + jnp.arange(count, dtype=jnp.int32)
        return gathered // share * rows + layer * share + gathered % share

    def first_fold(carry, piece, start):
        denom, pscore = carry
        score = jnp.dot(embed, piece.T, preferred_element_type=jnp.float32) * inv_temp
        ids = key_ids(start, piece.shape[0])
        weight = jnp.where(ids[None, :] == own_ids[:, None], 0.0, jnp.exp(score - inv_temp))
        hits = jnp.where(ids[None, :] == partner[:, None], score, 0.0)
        return (denom + jnp.sum(weight, axis=1), pscore + jnp.sum(hits, axis=1))

    empty_rows = jnp.zeros((rows,), jnp.float32)
    keys = lax.all_gather(mine, "batch", axis=0, tiled=True)
    group = math.gcd(lax.axis_size("batch"), max(1, 512 // share))
    span = group * share
    turns = keys.shape[0] // span
    stacked = keys.reshape(turns, span, width)
    starts = jnp.arange(turns, dtype=jnp.int32) * span

    def first_step(carry, item):
        return (first_fold(carry, item[0], item[1]), None)

    (denom, pscore), unused = lax.scan(first_step, (empty_rows, empty_rows), (stacked, starts))
    denom, pscore = lax.psum((denom, pscore), "rep")
    lse = jnp.log(denom) + inv_temp
    loss = lse - pscore
    lse_share = lax.dynamic_slice_in_dim(lse, layer * share, share, 0)

    def second_fold(acc, pieces, start):
        piece, piece_lse = pieces
        score = jnp.dot(embed, piece.T, preferred_element_type=jnp.float32) * inv_temp
        ids = key_ids(start, piece.shape[0])
        coeff = jnp.exp(score - lse[:, None]) + jnp.exp(score - piece_lse[None, :])
        coeff = coeff - 2.0 * jnp.where(ids[None, :] == partner[:, None], 1.0, 0.0)
        coeff = jnp.where(ids[None, :] == own_ids[:, None], 0.0, coeff).astype(jnp.bfloat16)
        return acc + jnp.dot(coeff, piece, preferred_element_type=jnp.float32)

    empty_acc = jnp.zeros((rows, width), jnp.float32)
    key_lse = lax.all_gather(lse_share, "batch", axis=0, tiled=True)
    stacked_lse = key_lse.reshape(turns, span)

    def second_step(acc, item):
        return (second_fold(acc, (item[0], item[1]), item[2]), None)

    acc, unused = lax.scan(second_step, empty_acc, (stacked, stacked_lse, starts))
    total = lax.psum(acc, "rep")
    dz = total * inv_temp
    grad = scale * (dz - unit * jnp.sum(unit * dz, axis=-1, keepdims=True))
    return (grad, loss)


def solution(mesh):
    in_specs = (P("batch", None), P("batch"))
    out_specs = (P("batch", None), P("batch"))
    return jax.shard_map(
        on_device, mesh=mesh, in_specs=in_specs, out_specs=out_specs, check_vma=False
    )
```

profile of v0, /device:TPU:1, one launch (start us, length us, event | category | flops | bytes accessed | tf_op | source)
XLA Modules:
  0.0 2287.7 jit_solution(5188708973484321416)
XLA Ops:
  7.2 1.0 fusion.53
  8.2 1.0 fusion.49
  10.0 1.3 dynamic-slice
  11.9 902.2 %all-gather.2.cloned.1.call-done = bf16[6144,512]{1,0:T(8,128)(2,1)} async-done(((bf16[32,512]{1,0:T(8,128)(2,1)}), bf16[6144,512]{1,0:T(8,128)(2,1)}) %all-gather.2.cloned.1.call-update) | async-done | bytes 6291472 | tf_op jit(solution)/shard_map/all_gather | solution.py:37
  914.1 32.0 %while.28 = (s32[]{:T(128)}, f32[128]{0:T(128)S(1)}, f32[128]{0:T(128)S(1)}, s32[12]{0:T(128)S(1)}, s32[]{:T(128)}, /*index=5*/bf16[12,512,512]{2,1,0:T(8,128)(2...) while((s32[]{:T(128)}, f32[128]{0:T(128)S(1)}, ...), condition=%wide.region_4.5_spmd.clone, body=%wide.region_1.4_spmd.clone.sunk | while | flops 67645312 | bytes 665743 | solution.py:47
  914.7 0.7 fusion.65
  915.4 1.4 select_reduce_fusion.3
  917.4 0.7 fusion.65
  918.0 1.4 select_reduce_fusion.3
  920.0 0.7 fusion.65
  920.7 1.4 select_reduce_fusion.3
  923.4 1.4 select_reduce_fusion.3
  925.4 0.7 fusion.65
  926.1 1.4 select_reduce_fusion.3
  928.1 0.7 fusion.65
  928.7 1.4 select_reduce_fusion.3
  930.7 0.7 fusion.65
  931.4 1.4 select_reduce_fusion.3
  933.4 0.7 fusion.65
  934.1 1.4 select_reduce_fusion.3
  936.1 0.7 fusion.65
  936.8 1.4 select_reduce_fusion.3
  938.7 0.7 fusion.65
  939.4 1.4 select_reduce_fusion.3
  942.1 1.4 select_reduce_fusion.3
  944.1 0.7 fusion.65
  944.8 1.4 select_reduce_fusion.3
  946.2 153.2 %all-reduce.1 = (f32[128]{0:T(128)S(1)}, f32[128]{0:T(128)S(1)}) all-reduce(f32[128]{0:T(128)S(1)} %get-tuple-element.252, f32[128]{0:T(128)S(1)} %get-tuple-element.254), channel_id=1, replica_groups=mesh['batch'=192,'rep'=4] {'rep'}, use_global_device_ids=true, to_apply=%region_5.6 | all-reduce | flops 256 | bytes 2048 | tf_op jit(solution)/shard_map/psum | solution.py:48
  1100.1 918.7 %all-reduce = f32[6144]{0:T(1024)S(1)} all-reduce(f32[6144]{0:T(1024)S(1)} %dynamic-slice_dynamic-update-slice_fusion), channel_id=1, replica_groups=mesh['batch'=192,'rep'=4] {'batch'}, use_global_device_ids=true, to_apply=%add | all-reduce | flops 6144 | bytes 49152
  2018.8 38.7 %while.29 = (s32[]{:T(128)}, f32[128,512]{1,0:T(8,128)S(1)}, s32[12]{0:T(128)S(1)}, s32[]{:T(128)}, bf16[12,512,512]{2,1,0:T(8,128)(2,1)}, /*index=5*/bf16[128,5...) while((s32[]{:T(128)}, f32[128,512]{1,0:T(8,128)S(1)}, ...), condition=%wide.region_7.8_spmd.clone, body=%wide.region_6.7_spmd.clone.sunk | while | flops 135081600 | bytes 1717403 | solution.py:69
  2019.3 0.7 fusion.70
  2020.0 1.9 convolution_add_fusion.2
  2023.3 1.9 convolution_add_fusion.2
  2025.8 0.7 fusion.70
  2026.5 1.9 convolution_add_fusion.2
  2029.7 1.9 convolution_add_fusion.2
  2032.9 1.9 convolution_add_fusion.2
  2036.2 1.9 convolution_add_fusion.2
  2039.4 1.9 convolution_add_fusion.2
  2042.6 1.9 convolution_add_fusion.2
  2045.8 1.9 convolution_add_fusion.2
  2049.1 1.9 convolution_add_fusion.2
  2052.3 1.9 convolution_add_fusion.2
  2055.5 1.9 convolution_add_fusion.2
  2057.5 0.7 copy-done.1
  2058.2 219.8 %all-reduce.4.cloned.1.call-done = f32[128,512]{1,0:T(8,128)} async-done(((f32[128,512]{1,0:T(8,128)}), f32[128,512]{1,0:T(8,128)}) %all-reduce.4.cloned.1.call-update) | async-done | bytes 262160 | tf_op jit(solution)/shard_map/psum | solution.py:70
  2277.9 1.1 fusion.50
  2279.1 1.8 fusion.52
  (101 shorter events, 23.9 us)
Async XLA Ops:
  7.2 906.9 %all-gather.2.cloned.1.call-start = ((), (), s32[]{:S(2)}) async-start(), calls=%async_computation | async-start | bytes 6324224 | tf_op jit(solution)/shard_map/all_gather | solution.py:37
  9.9 2268.0 %all-reduce.4.cloned.1.call-start = ((), (), s32[]{:S(2)}) async-start(), calls=%async_computation.1 | async-start | bytes 524288 | tf_op jit(solution)/shard_map/psum | solution.py:70
  946.2 1331.8 %copy-start = (bf16[128,512]{1,0:T(8,128)(2,1)S(1)}, bf16[128,512]{1,0:T(8,128)(2,1)}, u32[]{:S(2)}) copy-start(bf16[128,512]{1,0:T(8,128)(2,1)} %param.6) | copy-start | bytes 393220
  2057.4 0.7 copy-start.1
Sparse Core Ops, SparseCore 0:
  10.9 903.1 all-gather.1
  2058.3 219.5 all-reduce.3
where the time goes:
time: 2290 us
  waiting for transfers between devices  1120 us (49%)
  blocking collectives  1070 us (47%)
  matrix products  39.4 us (2%)
    unnamed x1, blocking collectives  919 us
    all_gather x1, waiting for transfers between devices, on_device(): keys = lax.all_gather(mine, 'batch', axis=0, tiled=True)  902 us
    psum x1, waiting for transfers between devices, on_device(): total = lax.psum(acc, 'rep')  220 us
    psum x1, blocking collectives, on_device(): denom, pscore = lax.psum((denom, pscore), 'rep')  153 us
  transfers between devices with their start and end apart: 2, of which 2 were waited for; matrix products, arithmetic and copies ran while one was open for 0% of the time, Pallas kernels for 0%

commit v1 on v0

v1 whole, which is shorter than its diff:
```python
import jax
import jax.numpy as jnp
from jax import lax
from jax.experimental import pallas as pl
from jax.experimental.pallas import tpu as pltpu
from jax.sharding import PartitionSpec as P

MESH = pl.DeviceIdType.MESH
F32 = jnp.float32
BF16 = jnp.bfloat16

NX, NY, NZ = 4, 8, 12
NQ = 4
PLANE = NX * NQ
ROWS, WIDTH = 128, 512
HALF = ROWS // 2
NR = PLANE * HALF
TILE = 256


def kernel(
    feats_ref,
    partner_ref,
    grad_ref,
    loss_ref,
    rows,
    cols,
    colp,
    ebuf,
    dacc,
    pacc,
    rsend,
    rmsg,
    csend,
    cmsg,
    rcol,
    square,
    rrow,
    coeff,
    psend,
    prec,
    row_s,
    row_r,
    ring_s,
    ring_r,
    pair_s,
    pair_r,
    part_s,
    part_r,
    sum_s,
    sum_r,
    den_s,
    den_r,
    dz_s,
    dz_r,
    fin_s,
    fin_r,
):
    block = lax.axis_index("batch")
    layer = lax.axis_index("rep")
    x = block % NX
    z = (block // NX) % NZ
    q = block // (NX * NZ)
    core = layer % 2
    y = (layer // 2) * NQ + q
    mine = q * NX + x

    def device(dx, dy, dz, flip):
        ny = (y + dy) % NY
        nz = (z + dz) % NZ
        nx = (x + dx) % NX
        return ((ny % NQ) * (NX * NZ) + nz * NX + nx, (ny // NQ) * 2 + (core + flip) % 2)

    def y_step(dyi):
        return dyi + (dyi // 3) * 4 + (dyi // 2 - dyi // 3) * 4 * core

    def plane_dest(i):
        return device(i % NX, y_step(i // NX), 0, 0)

    def plane_source(i):
        return device(NX - i % NX, NY - y_step(i // NX), 0, 0)

    def plane_dest_slot(i):
        return ((q + i // NX) % NQ) * NX + (x + i % NX) % NX

    barrier = pltpu.get_barrier_semaphore()

    def greet_plane(i, carry):
        pl.semaphore_signal(barrier, inc=1, device_id=plane_source(i), device_id_type=MESH)
        return carry

    def greet_line(i, carry):
        pl.semaphore_signal(
            barrier, inc=1, device_id=device(0, 0, i // 2, i % 2), device_id_type=MESH
        )
        return carry

    lax.fori_loop(1, PLANE, greet_plane, 0)
    lax.fori_loop(1, 2 * NZ, greet_line, 0)

    hf = feats_ref[...].astype(F32)
    scale = lax.rsqrt(jnp.sum(hf * hf, axis=-1, keepdims=True) + 1e-06)
    embed = (hf * scale).astype(BF16)
    cols[z] = embed
    colp[z] = partner_ref[...]
    half = pl.multiple_of(core * HALF, HALF)
    rows[mine] = cols[z, pl.ds(half, HALF), :]

    pl.semaphore_wait(barrier, PLANE - 1 + 2 * NZ - 1)

    ahead = 1 + (NZ - 2) * core

    def ring_copy(k, h):
        src = (z + (NZ - ahead) * (k - 1)) % NZ
        part = cols.at[src, pl.ds(h * HALF, HALF)]
        n = (k - 1) * 2 + h
        return pltpu.make_async_remote_copy(
            src_ref=part,
            dst_ref=part,
            send_sem=ring_s.at[n],
            recv_sem=ring_r.at[n],
            device_id=device(0, 0, ahead, 0),
            device_id_type=MESH,
        )

    def ring_last():
        src = (z + (NZ - ahead) * (NZ // 2 - 1)) % NZ
        part = cols.at[src, pl.ds(half, HALF)]
        return pltpu.make_async_remote_copy(
            src_ref=part,
            dst_ref=part,
            send_sem=ring_s.at[10],
            recv_sem=ring_r.at[10],
            device_id=device(0, 0, ahead, 0),
            device_id_type=MESH,
        )

    def pair_copy(k, h, n):
        src = (z + (NZ - ahead) * k) % NZ
        part = cols.at[src, pl.ds(pl.multiple_of(h * HALF, HALF), HALF)]
        return pltpu.make_async_remote_copy(
            src_ref=part,
            dst_ref=part,
            send_sem=pair_s.at[n],
            recv_sem=pair_r.at[n],
            device_id=device(0, 0, 0, 1),
            device_id_type=MESH,
        )

    def row_copy(i):
        return pltpu.make_async_remote_copy(
            src_ref=cols.at[z, pl.ds(half, HALF)],
            dst_ref=rows.at[mine],
            send_sem=row_s.at[i],
            recv_sem=row_r.at[i],
            device_id=plane_dest(i),
            device_id_type=MESH,
        )

    def partner_copy(i):
        return pltpu.make_async_remote_copy(
            src_ref=partner_ref,
            dst_ref=colp.at[z],
            send_sem=part_s.at[i],
            recv_sem=part_r.at[i],
            device_id=device(0, 0, i, 0),
            device_id_type=MESH,
        )

    def start(make):
        def body(i, carry):
            make(i).start()
            return carry

        return body

    def wait_recv(make):
        def body(i, carry):
            make(i).wait_recv()
            return carry

        return body

    def wait_send(make):
        def body(i, carry):
            make(i).wait_send()
            return carry

        return body

    for h in range(2):
        ring_copy(1, h).start()
    lax.fori_loop(1, PLANE, start(row_copy), 0)
    lax.fori_loop(1, NZ, start(partner_copy), 0)

    for k in range(1, 6):
        for h in range(2):
            ring_copy(k, h).wait_recv()
            if k < 5:
                ring_copy(k + 1, h).start()
            pair_copy(k, h, (k - 1) * 2 + h).start()
    ring_last().start()
    lax.fori_loop(1, PLANE, wait_recv(row_copy), 0)
    lax.fori_loop(1, NZ, wait_recv(partner_copy), 0)
    ring_last().wait_recv()
    pair_copy(6, core, 10).start()
    for n in range(11):
        pair_copy(1, 0, n).wait_recv()

    lane = lax.broadcasted_iota(jnp.int32, (1, TILE), 1)
    row_in_tile = lax.broadcasted_iota(jnp.int32, (TILE, 1), 0)

    def row_ids(t):
        return (t * NZ * NX + z * NX) * ROWS + core * HALF + (row_in_tile // HALF) * HALF + row_in_tile

    def mates(k):
        return jnp.concatenate([colp[2 * k], colp[2 * k + 1]], axis=1)

    dacc[...] = jnp.zeros_like(dacc)
    pacc[...] = jnp.zeros_like(pacc)

    def score_step(k, carry):
        keys = cols[pl.ds(2 * k, 2)].reshape(TILE, WIDTH)
        key_ids = (q * NZ * NX + (2 * k + lane // ROWS) * NX + x) * ROWS + lane % ROWS
        mate = mates(k)
        for t in range(NQ):
            ids = row_ids(t)
            span = pl.ds(t * TILE, TILE)
            score = lax.dot_general(
                rows[pl.ds(t * NX, NX)].reshape(TILE, WIDTH),
                keys,
                (((1,), (1,)), ((), ())),
                preferred_element_type=F32,
            ) * 10.0
            weight = jnp.where(key_ids == ids, 0.0, jnp.exp(score - 10.0))
            hits = jnp.where(mate == ids, score, 0.0)
            ebuf[k, span] = weight
            dacc[span] += weight[:, :ROWS] + weight[:, ROWS:]
            pacc[span] += hits[:, :ROWS] + hits[:, ROWS:]
        return carry

    lax.fori_loop(0, NZ // 2, score_step, 0)

    for g in range(8):
        span = pl.ds(g * ROWS, ROWS)
        rsend[pl.ds(g, 1)] = jnp.sum(dacc[span].T, axis=0, keepdims=True)
        rsend[pl.ds(8 + g, 1)] = jnp.sum(pacc[span].T, axis=0, keepdims=True)
    rmsg[mine] = rsend[...]

    def sum_copy(i):
        return pltpu.make_async_remote_copy(
            src_ref=rsend,
            dst_ref=rmsg.at[mine],
            send_sem=sum_s.at[i],
            recv_sem=sum_r.at[i],
            device_id=plane_dest(i),
            device_id_type=MESH,
        )

    lax.fori_loop(1, PLANE, start(sum_copy), 0)
    lax.fori_loop(1, PLANE, wait_recv(sum_copy), 0)
    total = rmsg[0]
    for p in range(1, PLANE):
        total = total + rmsg[p]
    square[pl.ds(0, 16)] = total

    low = lax.broadcasted_iota(jnp.int32, (1, ROWS), 1) < HALF
    own_den = square[pl.ds(mine // 2, 1)]
    own_pos = square[pl.ds(8 + mine // 2, 1)]
    odd = mine % 2 == 1
    own_den = jnp.where(odd, pltpu.roll(own_den, HALF, 1), own_den)
    own_pos = jnp.where(odd, own_pos, pltpu.roll(own_pos, HALF, 1))
    note = jnp.where(low, own_den, own_pos)
    csend[...] = note
    cmsg[2 * z + core] = note

    def den_copy(i):
        return pltpu.make_async_remote_copy(
            src_ref=csend,
            dst_ref=cmsg.at[2 * z + core],
            send_sem=den_s.at[i],
            recv_sem=den_r.at[i],
            device_id=device(0, 0, i // 2, i % 2),
            device_id_type=MESH,
        )

    lax.fori_loop(1, 2 * NZ, start(den_copy), 0)

    square[pl.ds(0, 8)] = 1.0 / total[:8]
    turned = square[...].T
    for g in range(8):
        rrow[pl.ds(g * ROWS, ROWS)] = jnp.broadcast_to(turned[:, g : g + 1], (ROWS, ROWS))

    lax.fori_loop(1, 2 * NZ, wait_recv(den_copy), 0)

    def den_of(j):
        return jnp.where(low, cmsg[2 * j], pltpu.roll(cmsg[2 * j + 1], HALF, 1))

    for j in range(NZ):
        rcol[j] = 1.0 / den_of(j)
    pos = jnp.where(low, pltpu.roll(cmsg[2 * z], HALF, 1), cmsg[2 * z + 1])
    loss_ref[...] = jnp.log(den_of(z)) + 10.0 - pos

    def dz_copy(i):
        return pltpu.make_async_remote_copy(
            src_ref=psend.at[plane_dest_slot(i)],
            dst_ref=prec.at[mine],
            send_sem=dz_s.at[i],
            recv_sem=dz_r.at[i],
            device_id=plane_dest(i),
            device_id_type=MESH,
        )

    keys_all = cols[...].reshape(NZ * ROWS, WIDTH)
    for turn in (2, 1, 3, 0):
        t = (q + turn) % NQ
        ids = row_ids(t)
        span = pl.ds(pl.multiple_of(t * TILE, TILE), TILE)
        row_part = rrow[span]
        row_part = jnp.concatenate([row_part, row_part], axis=1)

        def coeff_step(k, carry):
            col_part = jnp.concatenate([rcol[2 * k], rcol[2 * k + 1]], axis=1)
            value = ebuf[k, span] * (row_part + col_part)
            value = value - jnp.where(mates(k) == ids, 2.0, 0.0)
            coeff[:, pl.ds(pl.multiple_of(k * TILE, TILE), TILE)] = value.astype(BF16)
            return carry

        for k in range(NZ // 2):
            coeff_step(k, 0)
        dz = jnp.dot(coeff[...], keys_all, preferred_element_type=F32)
        psend[pl.ds(t * NX, NX)] = dz.astype(BF16).reshape(NX, HALF, WIDTH)
        if turn == 0:
            prec[mine] = psend[mine]
        lax.fori_loop(max(1, turn * NX), turn * NX + NX, start(dz_copy), 0)

    lax.fori_loop(1, PLANE, wait_recv(dz_copy), 0)
    acc = prec[0].astype(F32)
    for p in range(1, PLANE):
        acc = acc + prec[p].astype(F32)
    acc = acc * 10.0
    hf = feats_ref[pl.ds(half, HALF)].astype(F32)
    scale = lax.rsqrt(jnp.sum(hf * hf, axis=-1, keepdims=True) + 1e-06)
    unit = hf * scale
    grad_ref[pl.ds(half, HALF)] = scale * (acc - unit * jnp.sum(unit * acc, axis=-1, keepdims=True))
    part = grad_ref.at[pl.ds(half, HALF)]
    last = pltpu.make_async_remote_copy(
        src_ref=part,
        dst_ref=part,
        send_sem=fin_s,
        recv_sem=fin_r,
        device_id=device(0, 0, 0, 1),
        device_id_type=MESH,
    )
    last.start()

    for k in range(1, 6):
        for h in range(2):
            ring_copy(k, h).wait_send()
    ring_last().wait_send()
    for n in range(11):
        pair_copy(1, 0, n).wait_send()
    lax.fori_loop(1, PLANE, wait_send(row_copy), 0)
    lax.fori_loop(1, NZ, wait_send(partner_copy), 0)
    lax.fori_loop(1, PLANE, wait_send(sum_copy), 0)
    lax.fori_loop(1, 2 * NZ, wait_send(den_copy), 0)
    lax.fori_loop(1, PLANE, wait_send(dz_copy), 0)
    last.wait()


def on_device(feats, partner):
    vmem = pl.BlockSpec(memory_space=pltpu.VMEM)
    dma = pltpu.SemaphoreType.DMA
    grad, loss = pl.pallas_call(
        kernel,
        out_shape=(
            jax.ShapeDtypeStruct((ROWS, WIDTH), F32),
            jax.ShapeDtypeStruct((1, ROWS), F32),
        ),
        in_specs=[vmem, vmem],
        out_specs=(vmem, vmem),
        scratch_shapes=[
            pltpu.VMEM((PLANE, HALF, WIDTH), BF16),
            pltpu.VMEM((NZ, ROWS, WIDTH), BF16),
            pltpu.VMEM((NZ, 1, ROWS), jnp.int32),
            pltpu.VMEM((NZ // 2, NR, TILE), F32),
            pltpu.VMEM((NR, ROWS), F32),
            pltpu.VMEM((NR, ROWS), F32),
            pltpu.VMEM((16, ROWS), F32),
            pltpu.VMEM((PLANE, 16, ROWS), F32),
            pltpu.VMEM((1, ROWS), F32),
            pltpu.VMEM((2 * NZ, 1, ROWS), F32),
            pltpu.VMEM((NZ, 1, ROWS), F32),
            pltpu.VMEM((ROWS, ROWS), F32),
            pltpu.VMEM((NR, ROWS), F32),
            pltpu.VMEM((TILE, NZ * ROWS), BF16),
            pltpu.VMEM((PLANE, HALF, WIDTH), BF16),
            pltpu.VMEM((PLANE, HALF, WIDTH), BF16),
            dma((PLANE,)),
            dma((PLANE,)),
            dma((11,)),
            dma((11,)),
            dma((11,)),
            dma((11,)),
            dma((NZ,)),
            dma((NZ,)),
            dma((PLANE,)),
            dma((PLANE,)),
            dma((2 * NZ,)),
            dma((2 * NZ,)),
            dma((PLANE,)),
            dma((PLANE,)),
            dma,
            dma,
        ],
        compiler_params=pltpu.CompilerParams(
            collective_id=0, has_side_effects=True, vmem_limit_bytes=48 * 2**20
        ),
    )(feats, partner.reshape(1, ROWS))
    return grad, loss.reshape(ROWS)


def solution(mesh):
    in_specs = (P("batch", None), P("batch"))
    out_specs = (P("batch", None), P("batch"))
    return jax.shard_map(
        on_device, mesh=mesh, in_specs=in_specs, out_specs=out_specs, check_vma=False
    )
```

time: 2290 us -> 81 us (0.04)
  waiting for transfers between devices: 1120 us -> 0 us
  blocking collectives: 1070 us -> 0 us
  Pallas kernels: 0 us -> 77.4 us
  matrix products: 39.4 us -> 0 us
    unnamed x1 -> x0, blocking collectives: 919 us -> none
    all_gather x1 -> x0, waiting for transfers between devices: 902 us -> none  [on_device(): keys = lax.all_gather(mine, 'batch', axis=0, tiled=True)]
    psum x1 -> x0, waiting for transfers between devices: 220 us -> none  [on_device(): total = lax.psum(acc, 'rep')]
    psum x1 -> x0, blocking collectives: 153 us -> none  [on_device(): denom, pscore = lax.psum((denom, pscore), 'rep')]
    pallas_call x0 -> x1, Pallas kernels: none -> 77.4 us  [on_device(): pl.pallas_call(kernel, out_shape=(jax.ShapeDtypeStruct((ROWS, WIDTH), F32...]
    dot_general x24 -> x0, matrix products: 39.4 us -> none  [the longest x12 23 us: second_fold(): return acc + jnp.dot(coeff, piece, preferred_element_type=jnp.float32)]
  transfers between devices with their start and end apart: 2 -> 0, of which waited for: 2 -> 0; matrix products, arithmetic and copies ran while one was open for 0% -> 0% of each run, Pallas kernels for 0% -> 0%
where the time goes in v1:
time: 81 us; the launch traced here: 80.8 us
  Pallas kernels  77.4 us (96%)
  local copies, waits for them, and re-layouts  2.77 us (3%)
    pallas_call x1, Pallas kernels, on_device(): pl.pallas_call(kernel, out_shape=(jax.ShapeDtypeStruct((ROWS, WIDTH), F32...  77.4 us
    unnamed x6, local copies, waits for them, and re-layouts  2.77 us

profile of v1, /device:TPU:1, one launch (start us, length us, event | category | flops | bytes accessed | tf_op | source)
XLA Modules:
  0.0 80.8 jit_solution(8029931739210362085)
XLA Ops:
  0.6 0.0 copy-start.1
  0.6 0.6 copy-done.1
  1.3 0.0 copy-start
  1.3 0.9 %copy-done = bf16[128,512]{1,0:T(8,128)(2,1)S(1)} copy-done((bf16[128,512]{1,0:T(8,128)(2,1)S(1)}, bf16[128,512]{1,0:T(8,128)(2,1)}, u32[]{:S(2)}) %copy-start) | copy-done | bytes 131096
  2.2 77.4 %shard_map.41 = (f32[128,512]{1,0:T(8,128)S(1)}, f32[1,128]{1,0:T(1,128)S(1)}) custom-call(bf16[128,512]{1,0:T(8,128)(2,1)S(1)} %copy-done, s32[1,128]{1,0:T(1,128)S(1)} %bitcast.2), custom_call_target="tpu_custom_call" | custom-call | tf_op jit(solution)/shard_map/pallas_call | solution.py:374
  79.6 0.7 copy.6
  80.3 0.5 copy.7
Async XLA Ops:
  0.6 0.7 copy-start.1
  1.3 0.9 %copy-start = (bf16[128,512]{1,0:T(8,128)(2,1)S(1)}, bf16[128,512]{1,0:T(8,128)(2,1)}, u32[]{:S(2)}) copy-start(bf16[128,512]{1,0:T(8,128)(2,1)} %feats_ref.1) | copy-start | bytes 393220

commit v2 on v0

v2 whole, which is shorter than its diff:
```python
import jax
import jax.numpy as jnp
from jax import lax
from jax.experimental import pallas as pl
from jax.experimental.pallas import tpu as pltpu
from jax.sharding import PartitionSpec as P

MESH = pl.DeviceIdType.MESH
F32 = jnp.float32
BF16 = jnp.bfloat16

NX, NY, NZ = 4, 8, 12
NQ = 4
PLANE = NX * NQ
ROWS, WIDTH = 128, 512
HALF = ROWS // 2
NR = PLANE * HALF
TILE = 256
CHUNKS = 4
CHUNK = ROWS // CHUNKS
NEAR = 9


def kernel(
    feats_hbm,
    partner_hbm,
    grad_ref,
    loss_ref,
    feats,
    rows,
    cols,
    colp,
    ebuf,
    dacc,
    rsend,
    rmsg,
    csend,
    cmsg,
    ssend,
    smsg,
    rcol,
    square,
    rrow,
    coeff,
    psend,
    prec,
    in_sem,
    row_s,
    row_r,
    ring_s,
    ring_r,
    pair_s,
    pair_r,
    part_s,
    part_r,
    sum_s,
    sum_r,
    near_s,
    near_r,
    far_s,
    far_r,
    pos_s,
    pos_r,
    dz_s,
    dz_r,
    fin_s,
    fin_r,
):
    block = lax.axis_index("batch")
    layer = lax.axis_index("rep")
    x = block % NX
    z = (block // NX) % NZ
    q = block // (NX * NZ)
    core = layer % 2
    y = (layer // 2) * NQ + q
    mine = q * NX + x

    def device(dx, dy, dz, flip):
        ny = (y + dy) % NY
        nz = (z + dz) % NZ
        nx = (x + dx) % NX
        return ((ny % NQ) * (NX * NZ) + nz * NX + nx, (ny // NQ) * 2 + (core + flip) % 2)

    def remote(src, dst, send_sem, recv_sem, target):
        return pltpu.make_async_remote_copy(
            src_ref=src,
            dst_ref=dst,
            send_sem=send_sem,
            recv_sem=recv_sem,
            device_id=target,
            device_id_type=MESH,
        )

    def y_step(dyi):
        return dyi + (dyi // 3) * 4 + (dyi // 2 - dyi // 3) * 4 * core

    def plane_dest(i):
        return device(i % NX, y_step(i // NX), 0, 0)

    def plane_source(i):
        return device(NX - i % NX, NY - y_step(i // NX), 0, 0)

    def plane_dest_slot(i):
        return ((q + i // NX) % NQ) * NX + (x + i % NX) % NX

    def line_dest(i):
        return device(0, 0, i // 2, i % 2)

    fetch = [
        pltpu.make_async_copy(feats_hbm, feats, in_sem.at[0]),
        pltpu.make_async_copy(partner_hbm, colp.at[0], in_sem.at[1]),
    ]
    for copy in fetch:
        copy.start()

    barrier = pltpu.get_barrier_semaphore()

    def greet_plane(i, carry):
        pl.semaphore_signal(barrier, inc=1, device_id=plane_source(i), device_id_type=MESH)
        return carry

    ahead = 1 + (NZ - 2) * core
    for dz, flip in ((NZ - ahead, 0), (ahead, 1), (0, 1)):
        pl.semaphore_signal(
            barrier, inc=1, device_id=device(0, 0, dz, flip), device_id_type=MESH
        )
    lax.fori_loop(1, PLANE, greet_plane, 0)
    for copy in fetch:
        copy.wait()

    hf = feats[...].astype(F32)
    scale = lax.rsqrt(jnp.sum(hf * hf, axis=-1, keepdims=True) + 1e-06)
    embed = (hf * scale).astype(BF16)
    cols[0] = embed
    half = pl.multiple_of(core * HALF, HALF)
    rows[mine] = cols[0, pl.ds(half, HALF), :]

    pl.semaphore_wait(barrier, PLANE - 1 + 3)

    LAST = NZ // 2

    def ring_slot(k):
        if k == 0:
            return 0
        return 1 if k == LAST else 2 * k + 1 - core

    def chunk_rows(h):
        return pl.ds(pl.multiple_of((2 * core + h) % CHUNKS * CHUNK, CHUNK), CHUNK)

    def ring_copy(k, h):
        n = (k - 1) * CHUNKS + h
        target = device(0, 0, ahead, 0)
        if k == LAST:
            target = device(0, 0, ahead, h // 2)
            h = h % 2
        return remote(
            cols.at[ring_slot(k - 1), chunk_rows(h)],
            cols.at[ring_slot(k), chunk_rows(h)],
            ring_s.at[n],
            ring_r.at[n],
            target,
        )

    def pair_copy(k):
        part = cols.at[ring_slot(k)]
        return remote(part, part, pair_s.at[k - 1], pair_r.at[k - 1], device(0, 0, 0, 1))

    def mate_copy(k):
        return remote(
            colp.at[ring_slot(k - 1)],
            colp.at[ring_slot(k)],
            part_s.at[k - 1],
            part_r.at[k - 1],
            device(0, 0, ahead, 0),
        )

    def mate_pair_copy(k):
        part = colp.at[ring_slot(k)]
        return remote(part, part, part_s.at[5 + k], part_r.at[5 + k], device(0, 0, 0, 1))

    def row_copy(i):
        return remote(
            cols.at[0, pl.ds(half, HALF)], rows.at[mine], row_s.at[i], row_r.at[i], plane_dest(i)
        )

    def slot_of(off):
        off = off % NZ
        if off in (0, LAST):
            return off // LAST
        return 2 * off if off < LAST else 2 * (NZ - off) + 1

    def loop(lo, hi, act):
        def body(i, carry):
            act(i)
            return carry

        lax.fori_loop(lo, hi, body, 0)

    pending = []

    def finish():
        for settle in pending:
            settle()

    for h in range(CHUNKS):
        ring_copy(1, h).start()
    mate_copy(1).start()
    for dyi in (0, 1, 3, 2):
        loop(max(1, dyi * NX), dyi * NX + NX, lambda i: row_copy(i).start())

    def settle_gather():
        for k in range(1, LAST + 1):
            for h in range(CHUNKS):
                ring_copy(k, h).wait_send()
            mate_copy(k).wait_send()
            if k < LAST:
                pair_copy(k).wait_send()
                mate_pair_copy(k).wait_send()
        loop(1, PLANE, lambda i: row_copy(i).wait_send())

    pending.append(settle_gather)

    def ring_step(k):
        for h in range(CHUNKS):
            ring_copy(k, h).wait_recv()
            if k < LAST - 1:
                ring_copy(k + 1, h).start()
            elif k == LAST - 1 and h < CHUNKS // 2:
                ring_copy(k + 1, h).start()
                ring_copy(k + 1, h + 2).start()
        mate_copy(k).wait_recv()
        if k < LAST:
            mate_copy(k + 1).start()
            pair_copy(k).start()
            mate_pair_copy(k).start()

    def pair_in(k):
        pair_copy(k).wait_recv()
        mate_pair_copy(k).wait_recv()

    def rows_in(turn):
        dyi = (NQ - turn) % NQ
        loop(max(1, dyi * NX), dyi * NX + NX, lambda i: row_copy(i).wait_recv())

    lane = lax.broadcasted_iota(jnp.int32, (1, ROWS), 1)
    row_in_tile = lax.broadcasted_iota(jnp.int32, (TILE, 1), 0)

    def row_ids(t):
        return (t * NZ * NX + z * NX) * ROWS + core * HALF + (row_in_tile // HALF) * HALF + row_in_tile

    def mates(j):
        return jnp.concatenate([colp[2 * j], colp[2 * j + 1]], axis=1)

    def score_of(t, keys):
        return lax.dot_general(
            rows[pl.ds(t * NX, NX)].reshape(TILE, WIDTH),
            keys,
            (((1,), (1,)), ((), ())),
            preferred_element_type=F32,
        ) * 10.0

    def place(slot):
        return slot - 1 if slot > 1 else slot * (NZ - 1)

    def sums(turn, slot, weight, hits):
        weight = jnp.sum(weight, axis=0, keepdims=True)
        hits = jnp.sum(hits, axis=0, keepdims=True)
        if turn == 0:
            csend[place(slot)] = weight
            ssend[place(slot)] = hits
        else:
            csend[place(slot)] += weight
            ssend[place(slot)] += hits

    def single(turn, slot):
        t = (q + turn) % NQ
        ids = row_ids(t)
        span = pl.ds(pl.multiple_of(t * TILE, TILE), TILE)
        score = score_of(t, cols[slot])
        weight = jnp.exp(score - 10.0)
        if slot == 0 and turn == 0:
            key_ids = block * ROWS + lane
            weight = jnp.where(key_ids == ids, 0.0, weight)
        hits = jnp.where(colp[slot] == ids, score, 0.0)
        ebuf[0, span, slot * ROWS : slot * ROWS + ROWS] = weight
        if slot == 0:
            dacc[span] = weight
        else:
            dacc[span] += weight
        sums(turn, slot, weight, hits)

    def pair(turn, j):
        t = (q + turn) % NQ
        ids = row_ids(t)
        span = pl.ds(pl.multiple_of(t * TILE, TILE), TILE)
        score = score_of(t, cols[2 * j : 2 * j + 2].reshape(TILE, WIDTH))
        weight = jnp.exp(score - 10.0)
        hits = jnp.where(mates(j) == ids, score, 0.0)
        ebuf[j, span] = weight
        dacc[span] += weight[:, :ROWS] + weight[:, ROWS:]
        for side in range(2):
            cut = slice(side * ROWS, side * ROWS + ROWS)
            sums(turn, 2 * j + side, weight[:, cut], hits[:, cut])

    def near_copy(i):
        return remote(
            csend.at[pl.ds(0, NEAR)],
            cmsg.at[i // 2 * 2 + core, pl.ds(0, NEAR)],
            near_s.at[i],
            near_r.at[i],
            line_dest(i),
        )

    def far_copy(i):
        return remote(
            csend.at[pl.ds(NEAR, NZ - NEAR)],
            cmsg.at[i // 2 * 2 + core, pl.ds(NEAR, NZ - NEAR)],
            far_s.at[i],
            far_r.at[i],
            line_dest(i),
        )

    ring_step(1)
    ring_step(2)
    ring_step(3)
    rows_in(0)
    single(0, 0)
    pair_in(1)
    pair(0, 1)
    pair_in(2)
    pair(0, 2)
    ring_step(4)
    rows_in(3)
    rows_in(1)
    for turn in (1, 3):
        single(turn, 0)
        pair(turn, 1)
    pair_in(3)
    pair(0, 3)
    ring_step(5)
    for turn in (1, 3):
        pair(turn, 2)
        pair(turn, 3)
    pair_in(4)
    for turn in (0, 1, 3):
        pair(turn, 4)
    rows_in(2)
    single(2, 0)
    for j in range(1, 5):
        pair(2, j)
    pair_in(5)
    pair(0, 5)
    pair(1, 5)
    ring_step(6)
    loop(1, 2 * NZ, lambda i: near_copy(i).start())
    pending.append(lambda: loop(1, 2 * NZ, lambda i: near_copy(i).wait_send()))
    pair(2, 5)
    pair(3, 5)
    for turn in range(NQ):
        single(turn, 1)

    loop(1, 2 * NZ, lambda i: far_copy(i).start())
    pending.append(lambda: loop(1, 2 * NZ, lambda i: far_copy(i).wait_send()))

    for g in range(8):
        span = pl.ds(g * ROWS, ROWS)
        rsend[pl.ds(g, 1)] = jnp.sum(dacc[span].T, axis=0, keepdims=True)

    def sum_copy(i):
        return remote(rsend, rmsg.at[mine], sum_s.at[i], sum_r.at[i], plane_dest(i))

    loop(1, PLANE, lambda i: sum_copy(i).start())
    pending.append(lambda: loop(1, PLANE, lambda i: sum_copy(i).wait_send()))

    def pos_copy(d, flip):
        n = 2 * d + flip
        return remote(
            ssend.at[place(slot_of(d))],
            smsg.at[2 * d + core],
            pos_s.at[n],
            pos_r.at[n],
            device(0, 0, d, flip),
        )

    others = [(d, flip) for d in range(NZ) for flip in range(2) if d + flip]
    for d, flip in others:
        pos_copy(d, flip).start()
    pending.append(lambda: [pos_copy(d, flip).wait_send() for d, flip in others])

    rmsg[mine] = rsend[...]
    cmsg[core] = csend[...]
    smsg[core] = ssend[0]
    loop(1, PLANE, lambda i: sum_copy(i).wait_recv())
    total = rmsg[0]
    for p in range(1, PLANE):
        total = total + rmsg[p]
    square[pl.ds(0, 8)] = 1.0 / total
    turned = square[...].T
    for g in range(8):
        rrow[pl.ds(g * ROWS, ROWS)] = jnp.broadcast_to(turned[:, g : g + 1], (ROWS, ROWS))

    loop(1, 2 * NZ, lambda i: near_copy(i).wait_recv())
    loop(1, 2 * NZ, lambda i: far_copy(i).wait_recv())
    own_den = None
    for off in range(NZ):
        den = None
        for d in range(NZ):
            for c in range(2):
                part = cmsg[2 * d + c, place(slot_of(off + d))]
                den = part if den is None else den + part
        rcol[slot_of(off)] = 1.0 / den
        if off == 0:
            own_den = den
    loss_ref[...] = jnp.log(own_den) + 10.0

    def dz_copy(i):
        return remote(
            psend.at[plane_dest_slot(i)], prec.at[mine], dz_s.at[i], dz_r.at[i], plane_dest(i)
        )

    keys_all = cols[...].reshape(NZ * ROWS, WIDTH)
    for turn in (2, 1, 3, 0):
        t = (q + turn) % NQ
        ids = row_ids(t)
        span = pl.ds(pl.multiple_of(t * TILE, TILE), TILE)
        row_part = rrow[span]
        row_part = jnp.concatenate([row_part, row_part], axis=1)
        for j in range(NZ // 2):
            col_part = jnp.concatenate([rcol[2 * j], rcol[2 * j + 1]], axis=1)
            value = ebuf[j, span] * (row_part + col_part)
            value = value - jnp.where(mates(j) == ids, 2.0, 0.0)
            coeff[:, j * TILE : j * TILE + TILE] = value.astype(BF16)
        dz = jnp.dot(coeff[...], keys_all, preferred_element_type=F32)
        psend[pl.ds(t * NX, NX)] = dz.astype(BF16).reshape(NX, HALF, WIDTH)
        if turn == 0:
            prec[mine] = psend[mine]
        loop(max(1, turn * NX), turn * NX + NX, lambda i: dz_copy(i).start())
    pending.append(lambda: loop(1, PLANE, lambda i: dz_copy(i).wait_send()))

    for d, flip in others:
        pos_copy(d, flip).wait_recv()
    pos = smsg[0]
    for n in range(1, 2 * NZ):
        pos = pos + smsg[n]
    loss_ref[...] -= pos

    loop(1, PLANE, lambda i: dz_copy(i).wait_recv())
    acc = prec[0].astype(F32)
    for p in range(1, PLANE):
        acc = acc + prec[p].astype(F32)
    acc = acc * 10.0
    hf = feats[pl.ds(half, HALF)].astype(F32)
    scale = lax.rsqrt(jnp.sum(hf * hf, axis=-1, keepdims=True) + 1e-06)
    unit = hf * scale
    grad_ref[pl.ds(half, HALF)] = scale * (acc - unit * jnp.sum(unit * acc, axis=-1, keepdims=True))
    part = grad_ref.at[pl.ds(half, HALF)]
    last = remote(part, part, fin_s, fin_r, device(0, 0, 0, 1))
    last.start()
    finish()
    last.wait()


def on_device(feats, partner):
    vmem = pl.BlockSpec(memory_space=pltpu.VMEM)
    hbm = pl.BlockSpec(memory_space=pltpu.HBM)
    dma = pltpu.SemaphoreType.DMA
    grad, loss = pl.pallas_call(
        kernel,
        out_shape=(
            jax.ShapeDtypeStruct((ROWS, WIDTH), F32),
            jax.ShapeDtypeStruct((1, ROWS), F32),
        ),
        in_specs=[hbm, hbm],
        out_specs=(vmem, vmem),
        scratch_shapes=[
            pltpu.VMEM((ROWS, WIDTH), BF16),
            pltpu.VMEM((PLANE, HALF, WIDTH), BF16),
            pltpu.VMEM((NZ, ROWS, WIDTH), BF16),
            pltpu.VMEM((NZ, 1, ROWS), jnp.int32),
            pltpu.VMEM((NZ // 2, NR, TILE), F32),
            pltpu.VMEM((NR, ROWS), F32),
            pltpu.VMEM((8, ROWS), F32),
            pltpu.VMEM((PLANE, 8, ROWS), F32),
            pltpu.VMEM((NZ, 1, ROWS), F32),
            pltpu.VMEM((2 * NZ, NZ, 1, ROWS), F32),
            pltpu.VMEM((NZ, 1, ROWS), F32),
            pltpu.VMEM((2 * NZ, 1, ROWS), F32),
            pltpu.VMEM((NZ, 1, ROWS), F32),
            pltpu.VMEM((ROWS, ROWS), F32),
            pltpu.VMEM((NR, ROWS), F32),
            pltpu.VMEM((TILE, NZ * ROWS), BF16),
            pltpu.VMEM((PLANE, HALF, WIDTH), BF16),
            pltpu.VMEM((PLANE, HALF, WIDTH), BF16),
            dma((2,)),
        ]
        + [dma((PLANE,))] * 2
        + [dma((6 * CHUNKS,))] * 2
        + [dma((6,))] * 2
        + [dma((NZ,))] * 2
        + [dma((PLANE,))] * 2
        + [dma((2 * NZ,))] * 6
        + [dma((PLANE,))] * 2
        + [dma] * 2,
        compiler_params=pltpu.CompilerParams(
            collective_id=0, has_side_effects=True
        ),
    )(feats, partner.reshape(1, ROWS))
    return grad, loss.reshape(ROWS)


def solution(mesh):
    in_specs = (P("batch", None), P("batch"))
    out_specs = (P("batch", None), P("batch"))
    return jax.shard_map(
        on_device, mesh=mesh, in_specs=in_specs, out_specs=out_specs, check_vma=False
    )
```

time: 2290 us -> 73.6 us (0.03)
  waiting for transfers between devices: 1120 us -> 0 us
  blocking collectives: 1070 us -> 0 us
  Pallas kernels: 0 us -> 70.6 us
  matrix products: 39.4 us -> 0 us
    unnamed x1 -> x0, blocking collectives: 919 us -> none
    all_gather x1 -> x0, waiting for transfers between devices: 902 us -> none  [on_device(): keys = lax.all_gather(mine, 'batch', axis=0, tiled=True)]
    psum x1 -> x0, waiting for transfers between devices: 220 us -> none  [on_device(): total = lax.psum(acc, 'rep')]
    psum x1 -> x0, blocking collectives: 153 us -> none  [on_device(): denom, pscore = lax.psum((denom, pscore), 'rep')]
    pallas_call x0 -> x1, Pallas kernels: none -> 70.6 us  [on_device(): pl.pallas_call(kernel, out_shape=(jax.ShapeDtypeStruct((ROWS, WIDTH), F32...]
    dot_general x24 -> x0, matrix products: 39.4 us -> none  [the longest x12 23 us: second_fold(): return acc + jnp.dot(coeff, piece, preferred_element_type=jnp.float32)]
  transfers between devices with their start and end apart: 2 -> 0, of which waited for: 2 -> 0; matrix products, arithmetic and copies ran while one was open for 0% -> 0% of each run, Pallas kernels for 0% -> 0%
where the time goes in v2:
time: 73.6 us; the launch traced here: 73.4 us
  Pallas kernels  70.6 us (96%)
  local copies, waits for them, and re-layouts  2.19 us (3%)
    pallas_call x1, Pallas kernels, on_device(): pl.pallas_call(kernel, out_shape=(jax.ShapeDtypeStruct((ROWS, WIDTH), F32...  70.6 us
    unnamed x4, local copies, waits for them, and re-layouts  2.19 us

profile of v2, /device:TPU:1, one launch (start us, length us, event | category | flops | bytes accessed | tf_op | source)
XLA Modules:
  0.0 73.4 jit_solution(488111921535583358)
XLA Ops:
  0.6 70.6 %shard_map.41 = (f32[128,512]{1,0:T(8,128)}, f32[1,128]{1,0:T(1,128)}) custom-call(bf16[128,512]{1,0:T(8,128)(2,1)} %feats_hbm.1, s32[1,128]{1,0:T(1,128)} %bitcast.2), custom_call_target="tpu_custom_call" | custom-call | tf_op jit(solution)/shard_map/pallas_call | solution.py:467
  71.2 0.0 copy-start
  71.2 1.7 %copy.6 = f32[128,512]{1,0:T(8,128)} copy(f32[128,512]{1,0:T(8,128)} %get-tuple-element.8) | data formatting | bytes 524288
  72.9 0.0 copy-done
  72.9 0.5 copy.7
Async XLA Ops:
  71.2 1.7 %copy-start = (f32[1,128]{1,0:T(1,128)S(1)}, f32[1,128]{1,0:T(1,128)}, u32[]{:S(2)}) copy-start(f32[1,128]{1,0:T(1,128)} %get-tuple-element.5) | copy-start | bytes 1540

commit v3 on v2

--- a/solution.py
+++ b/solution.py
@@ -44,6 +44,7 @@
     coeff,
     psend,
     prec,
+    final,
     in_sem,
     row_s,
     row_r,
@@ -349,13 +350,13 @@
     for j in range(1, 5):
         pair(2, j)
     pair_in(5)
-    pair(0, 5)
-    pair(1, 5)
+    loop(1, NZ, lambda i: near_copy(i).start())
+    loop(NZ + 2, 2 * NZ, lambda i: near_copy(i).start())
+    pending.append(lambda: loop(1, 2 * NZ, lambda i: near_copy(i).wait_send()))
+    for turn in range(NQ):
+        pair(turn, 5)
     ring_step(6)
-    loop(1, 2 * NZ, lambda i: near_copy(i).start())
-    pending.append(lambda: loop(1, 2 * NZ, lambda i: near_copy(i).wait_send()))
-    pair(2, 5)
-    pair(3, 5)
+    loop(NZ, NZ + 2, lambda i: near_copy(i).start())
     for turn in range(NQ):
         single(turn, 1)
 
@@ -434,7 +435,9 @@
         psend[pl.ds(t * NX, NX)] = dz.astype(BF16).reshape(NX, HALF, WIDTH)
         if turn == 0:
             prec[mine] = psend[mine]
-        loop(max(1, turn * NX), turn * NX + NX, lambda i: dz_copy(i).start())
+        for dx in (2, 1, 3, 0):
+            if turn + dx:
+                dz_copy(turn * NX + dx).start()
     pending.append(lambda: loop(1, PLANE, lambda i: dz_copy(i).wait_send()))
 
     for d, flip in others:
@@ -452,11 +455,14 @@
     hf = feats[pl.ds(half, HALF)].astype(F32)
     scale = lax.rsqrt(jnp.sum(hf * hf, axis=-1, keepdims=True) + 1e-06)
     unit = hf * scale
-    grad_ref[pl.ds(half, HALF)] = scale * (acc - unit * jnp.sum(unit * acc, axis=-1, keepdims=True))
+    final[...] = scale * (acc - unit * jnp.sum(unit * acc, axis=-1, keepdims=True))
     part = grad_ref.at[pl.ds(half, HALF)]
-    last = remote(part, part, fin_s, fin_r, device(0, 0, 0, 1))
+    last = remote(final, part, fin_s, fin_r, device(0, 0, 0, 1))
     last.start()
+    keep = pltpu.make_async_copy(final, part, in_sem.at[0])
+    keep.start()
     finish()
+    keep.wait()
     last.wait()
 
 
@@ -471,7 +477,7 @@
             jax.ShapeDtypeStruct((1, ROWS), F32),
         ),
         in_specs=[hbm, hbm],
-        out_specs=(vmem, vmem),
+        out_specs=(hbm, vmem),
         scratch_shapes=[
             pltpu.VMEM((ROWS, WIDTH), BF16),
             pltpu.VMEM((PLANE, HALF, WIDTH), BF16),
@@ -491,6 +497,7 @@
             pltpu.VMEM((TILE, NZ * ROWS), BF16),
             pltpu.VMEM((PLANE, HALF, WIDTH), BF16),
             pltpu.VMEM((PLANE, HALF, WIDTH), BF16),
+            pltpu.VMEM((HALF, WIDTH), F32),
             dma((2,)),
         ]
         + [dma((PLANE,))] * 2

time: 73.6 us -> 70.8 us (0.962)
  Pallas kernels: 70.6 us -> 67.8 us
    pallas_call x1, Pallas kernels: 70.6 us -> 67.8 us  [on_device(): pl.pallas_call(kernel, out_shape=(jax.ShapeDtypeStruct((ROWS, WIDTH), F32...]
where the time goes in v3:
time: 70.8 us; the launch traced here: 70.6 us
  Pallas kernels  67.8 us (96%)
  local copies, waits for them, and re-layouts  2.19 us (3%)
    pallas_call x1, Pallas kernels, on_device(): pl.pallas_call(kernel, out_shape=(jax.ShapeDtypeStruct((ROWS, WIDTH), F32...  67.8 us
    unnamed x4, local copies, waits for them, and re-layouts  2.19 us

profile of v3, /device:TPU:1, one launch (start us, length us, event | category | flops | bytes accessed | tf_op | source)
XLA Modules:
  0.0 70.6 jit_solution(14713225180186107976)
XLA Ops:
  0.6 67.8 %shard_map.41 = (f32[128,512]{1,0:T(8,128)}, f32[1,128]{1,0:T(1,128)}) custom-call(bf16[128,512]{1,0:T(8,128)(2,1)} %feats_hbm.1, s32[1,128]{1,0:T(1,128)} %bitcast.2), custom_call_target="tpu_custom_call" | custom-call | tf_op jit(solution)/shard_map/pallas_call | solution.py:473
  68.5 0.0 copy-start
  68.5 1.7 %copy.6 = f32[128,512]{1,0:T(8,128)} copy(f32[128,512]{1,0:T(8,128)} %get-tuple-element.8) | data formatting | bytes 524288
  70.1 0.0 copy-done
  70.1 0.5 copy.7
Async XLA Ops:
  68.5 1.7 %copy-start = (f32[1,128]{1,0:T(1,128)S(1)}, f32[1,128]{1,0:T(1,128)}, u32[]{:S(2)}) copy-start(f32[1,128]{1,0:T(1,128)} %get-tuple-element.5) | copy-start | bytes 1540

commit v4 on v3

--- a/solution.py
+++ b/solution.py
@@ -18,6 +18,7 @@
 TILE = 256
 CHUNKS = 4
 CHUNK = ROWS // CHUNKS
+FAR_FIRST = [2 * d + f for d in (6, 5, 7, 4, 8, 3, 9, 2, 10, 1, 11) for f in (0, 1)] + [1]
 NEAR = 9
 
 
@@ -69,18 +70,32 @@
 ):
     block = lax.axis_index("batch")
     layer = lax.axis_index("rep")
-    x = block % NX
-    z = (block // NX) % NZ
-    q = block // (NX * NZ)
-    core = layer % 2
-    y = (layer // 2) * NQ + q
+    x = lax.rem(block, NX)
+    z = lax.rem(lax.div(block, NX), NZ)
+    q = lax.div(block, NX * NZ)
+    core = lax.rem(layer, 2)
+    y = lax.div(layer, 2) * NQ + q
     mine = q * NX + x
 
     def device(dx, dy, dz, flip):
-        ny = (y + dy) % NY
-        nz = (z + dz) % NZ
-        nx = (x + dx) % NX
-        return ((ny % NQ) * (NX * NZ) + nz * NX + nx, (ny // NQ) * 2 + (core + flip) % 2)
+        return (plane_base(dx, dy) + line_base(dz), layer_base(dy) + side(flip))
+
+    def still(step):
+        return isinstance(step, int) and step == 0
+
+    def plane_base(dx, dy):
+        nx = x if still(dx) else lax.rem(x + dx, NX)
+        ny = q if still(dy) else lax.rem(q + dy, NQ)
+        return ny * (NX * NZ) + nx
+
+    def line_base(dz):
+        return (z if still(dz) else lax.rem(z + dz, NZ)) * NX
+
+    def layer_base(dy):
+        return layer - core if still(dy) else lax.div(lax.rem(y + dy, NY), NQ) * 2
+
+    def side(flip):
+        return core if still(flip) else 1 - core
 
     def remote(src, dst, send_sem, recv_sem, target):
         return pltpu.make_async_remote_copy(
@@ -93,16 +108,19 @@
         )
 
     def y_step(dyi):
+        if isinstance(dyi, int):
+            return (0, 1, 2 + 4 * core, 7)[dyi]
         return dyi + (dyi // 3) * 4 + (dyi // 2 - dyi // 3) * 4 * core
 
     def plane_dest(i):
         return device(i % NX, y_step(i // NX), 0, 0)
 
     def plane_source(i):
-        return device(NX - i % NX, NY - y_step(i // NX), 0, 0)
+        dx, dyi = i % NX, i // NX
+        return device((NX - dx) % NX, (0, 7, 6 - 4 * core, 1)[dyi], 0, 0)
 
     def plane_dest_slot(i):
-        return ((q + i // NX) % NQ) * NX + (x + i % NX) % NX
+        return lax.rem(q + i // NX, NQ) * NX + lax.rem(x + i % NX, NX)
 
     def line_dest(i):
         return device(0, 0, i // 2, i % 2)
@@ -116,16 +134,13 @@
 
     barrier = pltpu.get_barrier_semaphore()
 
-    def greet_plane(i, carry):
-        pl.semaphore_signal(barrier, inc=1, device_id=plane_source(i), device_id_type=MESH)
-        return carry
-
     ahead = 1 + (NZ - 2) * core
     for dz, flip in ((NZ - ahead, 0), (ahead, 1), (0, 1)):
         pl.semaphore_signal(
             barrier, inc=1, device_id=device(0, 0, dz, flip), device_id_type=MESH
         )
-    lax.fori_loop(1, PLANE, greet_plane, 0)
+    for i in range(1, PLANE):
+        pl.semaphore_signal(barrier, inc=1, device_id=plane_source(i), device_id_type=MESH)
     for copy in fetch:
         copy.wait()
 
@@ -207,7 +222,8 @@
         ring_copy(1, h).start()
     mate_copy(1).start()
     for dyi in (0, 1, 3, 2):
-        loop(max(1, dyi * NX), dyi * NX + NX, lambda i: row_copy(i).start())
+        for i in range(max(1, dyi * NX), dyi * NX + NX):
+            row_copy(i).start()
 
     def settle_gather():
         for k in range(1, LAST + 1):
@@ -350,17 +366,19 @@
     for j in range(1, 5):
         pair(2, j)
     pair_in(5)
-    loop(1, NZ, lambda i: near_copy(i).start())
-    loop(NZ + 2, 2 * NZ, lambda i: near_copy(i).start())
+    for i in FAR_FIRST[2:]:
+        near_copy(i).start()
     pending.append(lambda: loop(1, 2 * NZ, lambda i: near_copy(i).wait_send()))
     for turn in range(NQ):
         pair(turn, 5)
     ring_step(6)
-    loop(NZ, NZ + 2, lambda i: near_copy(i).start())
+    for i in FAR_FIRST[:2]:
+        near_copy(i).start()
     for turn in range(NQ):
         single(turn, 1)
 
-    loop(1, 2 * NZ, lambda i: far_copy(i).start())
+    for i in FAR_FIRST:
+        far_copy(i).start()
     pending.append(lambda: loop(1, 2 * NZ, lambda i: far_copy(i).wait_send()))
 
     for g in range(8):
@@ -370,7 +388,10 @@
     def sum_copy(i):
         return remote(rsend, rmsg.at[mine], sum_s.at[i], sum_r.at[i], plane_dest(i))
 
-    loop(1, PLANE, lambda i: sum_copy(i).start())
+    for dyi in (2, 1, 3, 0):
+        for dx in (2, 1, 3, 0):
+            if dyi + dx:
+                sum_copy(dyi * NX + dx).start()
     pending.append(lambda: loop(1, PLANE, lambda i: sum_copy(i).wait_send()))
 
     def pos_copy(d, flip):
@@ -384,9 +405,6 @@
         )
 
     others = [(d, flip) for d in range(NZ) for flip in range(2) if d + flip]
-    for d, flip in others:
-        pos_copy(d, flip).start()
-    pending.append(lambda: [pos_copy(d, flip).wait_send() for d, flip in others])
 
     rmsg[mine] = rsend[...]
     cmsg[core] = csend[...]
@@ -440,6 +458,9 @@
                 dz_copy(turn * NX + dx).start()
     pending.append(lambda: loop(1, PLANE, lambda i: dz_copy(i).wait_send()))
 
+    for d, flip in others:
+        pos_copy(d, flip).start()
+    pending.append(lambda: [pos_copy(d, flip).wait_send() for d, flip in others])
     for d, flip in others:
         pos_copy(d, flip).wait_recv()
     pos = smsg[0]

time: 70.8 us -> 69.4 us (0.980)
  Pallas kernels: 67.8 us -> 66.4 us
    pallas_call x1, Pallas kernels: 67.8 us -> 66.4 us  [on_device(): pl.pallas_call(kernel, out_shape=(jax.ShapeDtypeStruct((ROWS, WIDTH), F32...]
where the time goes in v4:
time: 69.4 us; the launch traced here: 69.2 us
  Pallas kernels  66.4 us (96%)
  local copies, waits for them, and re-layouts  2.19 us (3%)
    pallas_call x1, Pallas kernels, on_device(): pl.pallas_call(kernel, out_shape=(jax.ShapeDtypeStruct((ROWS, WIDTH), F32...  66.4 us
    unnamed x4, local copies, waits for them, and re-layouts  2.19 us

profile of v4, /device:TPU:1, one launch (start us, length us, event | category | flops | bytes accessed | tf_op | source)
XLA Modules:
  0.0 69.2 jit_solution(17994180641442787825)
XLA Ops:
  0.6 66.4 %shard_map.41 = (f32[128,512]{1,0:T(8,128)}, f32[1,128]{1,0:T(1,128)}) custom-call(bf16[128,512]{1,0:T(8,128)(2,1)} %feats_hbm.1, s32[1,128]{1,0:T(1,128)} %bitcast.2), custom_call_target="tpu_custom_call" | custom-call | tf_op jit(solution)/shard_map/pallas_call | solution.py:494
  67.0 0.0 copy-start
  67.1 1.7 %copy.6 = f32[128,512]{1,0:T(8,128)} copy(f32[128,512]{1,0:T(8,128)} %get-tuple-element.8) | data formatting | bytes 524288
  68.7 0.0 copy-done
  68.7 0.5 copy.7
Async XLA Ops:
  67.0 1.7 %copy-start = (f32[1,128]{1,0:T(1,128)S(1)}, f32[1,128]{1,0:T(1,128)}, u32[]{:S(2)}) copy-start(f32[1,128]{1,0:T(1,128)} %get-tuple-element.5) | copy-start | bytes 1540

commit v5 on v4

--- a/solution.py
+++ b/solution.py
@@ -451,8 +451,6 @@
             coeff[:, j * TILE : j * TILE + TILE] = value.astype(BF16)
         dz = jnp.dot(coeff[...], keys_all, preferred_element_type=F32)
         psend[pl.ds(t * NX, NX)] = dz.astype(BF16).reshape(NX, HALF, WIDTH)
-        if turn == 0:
-            prec[mine] = psend[mine]
         for dx in (2, 1, 3, 0):
             if turn + dx:
                 dz_copy(turn * NX + dx).start()
@@ -468,14 +466,18 @@
         pos = pos + smsg[n]
     loss_ref[...] -= pos
 
-    loop(1, PLANE, lambda i: dz_copy(i).wait_recv())
-    acc = prec[0].astype(F32)
-    for p in range(1, PLANE):
-        acc = acc + prec[p].astype(F32)
-    acc = acc * 10.0
     hf = feats[pl.ds(half, HALF)].astype(F32)
     scale = lax.rsqrt(jnp.sum(hf * hf, axis=-1, keepdims=True) + 1e-06)
-    unit = hf * scale
+    final[...] = hf * scale
+    acc = psend[mine].astype(F32)
+    for dyi in (2, 1, 3, 0):
+        for dx in (2, 1, 3, 0):
+            if dyi + dx:
+                dz_copy(dyi * NX + dx).wait_recv()
+                source = lax.rem(q + NQ - dyi, NQ) * NX + lax.rem(x + NX - dx, NX)
+                acc = acc + prec[source].astype(F32)
+    acc = acc * 10.0
+    unit = final[...]
     final[...] = scale * (acc - unit * jnp.sum(unit * acc, axis=-1, keepdims=True))
     part = grad_ref.at[pl.ds(half, HALF)]
     last = remote(final, part, fin_s, fin_r, device(0, 0, 0, 1))

time: 69.4 us -> 69.3 us (level)
  no operation moved by 1% of the time
where the time goes in v5:
time: 69.3 us; the launch traced here: 69.2 us
  Pallas kernels  66.3 us (96%)
  local copies, waits for them, and re-layouts  2.19 us (3%)
    pallas_call x1, Pallas kernels, on_device(): pl.pallas_call(kernel, out_shape=(jax.ShapeDtypeStruct((ROWS, WIDTH), F32...  66.3 us
    unnamed x4, local copies, waits for them, and re-layouts  2.19 us

profile of v5, /device:TPU:1, one launch (start us, length us, event | category | flops | bytes accessed | tf_op | source)
XLA Modules:
  0.0 69.2 jit_solution(8031541082400551428)
XLA Ops:
  0.6 66.3 %shard_map.41 = (f32[128,512]{1,0:T(8,128)}, f32[1,128]{1,0:T(1,128)}) custom-call(bf16[128,512]{1,0:T(8,128)(2,1)} %feats_hbm.1, s32[1,128]{1,0:T(1,128)} %bitcast.2), custom_call_target="tpu_custom_call" | custom-call | tf_op jit(solution)/shard_map/pallas_call | solution.py:496
  67.0 0.0 copy-start
  67.0 1.7 %copy.6 = f32[128,512]{1,0:T(8,128)} copy(f32[128,512]{1,0:T(8,128)} %get-tuple-element.8) | data formatting | bytes 524288
  68.7 0.0 copy-done
  68.7 0.5 copy.7
Async XLA Ops:
  67.0 1.7 %copy-start = (f32[1,128]{1,0:T(1,128)S(1)}, f32[1,128]{1,0:T(1,128)}, u32[]{:S(2)}) copy-start(f32[1,128]{1,0:T(1,128)} %get-tuple-element.5) | copy-start | bytes 1540
